TPU v7x, 1024 devices: a whole 8x8x8 slice. The times are simulated.
1024 devices in a mesh: rep: 32 (over y, x_hi, core), exp: 32 (over x_lo, z).
Axes of the slice: x: 8 (x_hi: 2, x_lo: 4; x = x_hi * 4 + x_lo), y: 8, z: 8, core: 2. Of those that a mesh axis runs over, the one named last changes fastest.
Arguments:
- replay_buffer_rows: bfloat16 [131072, 3584], P(('rep', 'exp')), may hold values from -6 to 6
- shard_request_index: int32 [1024, 32, 8], P(('rep', 'exp')), may hold values from 0 to 127
- replica_fetch_count: int32 [1024, 32], P(('rep', 'exp')), may hold values from 0 to 8, as said below
- routes: int32 [131072, 1], P(('rep', 'exp')), may hold values from 0 to 31; in each aligned block of 128 rows (0 to 127, 128 to 255, ...) at most 7 rows name the same one
- router_route_weight: float32 [131072, 1], P(('rep', 'exp')), may hold values from 0.25 to 1
- output_gradient: bfloat16 [131072, 1024], P(('rep', 'exp')), may hold values from -0.119628906 to 0.119628906
- frozen_gate_weight: bfloat16 [32, 3584, 1024], P('exp'), may hold values from -0.09375 to 0.09375
- adapter_down_weight: bfloat16 [32, 3584, 128], P('exp'), may hold values from -0.09375 to 0.09375
- adapter_up_weight: bfloat16 [32, 128, 1024], P('exp'), may hold values from -0.5 to 0.5
Outputs:
- out_rows: bfloat16 [131072, 1024], P(('rep', 'exp'))
- down_adapter_gradient: float32 [32, 3584, 128], P('exp', 'rep')
- up_adapter_gradient: float32 [32, 128, 1024], P('exp', 'rep')
Inputs may be any that keep to these rules, and one draw needn't show every extreme that they name: Each row replica_fetch_count[d, :] sums to 128, and every row has an entry equal to 8. `shard_request_index`: entry [s * 32 + c, r, j] is read only where j < replica_fetch_count[r * 32 + c, s]. `routes`: among the 128 rows of one device no expert is named more than 7 times, and that bound is reached.
All inputs are finite; a program needn't handle non-finite values.
Results may differ from a plain program's by a relative error of at most 0.0061.
Values may be sent and summed in bfloat16 or wider, within the bound.
A program may use at most 64 MiB of HBM per device.

v0:
```python
import jax
import jax.numpy as jnp
from jax import lax
from jax.sharding import PartitionSpec as P


def silu_slope(pre_act):
    gate_value = jax.nn.sigmoid(pre_act)
    return gate_value * (1.0 + pre_act * (1.0 - gate_value))


def body(
    replay_buffer_rows,
    shard_request_index,
    replica_fetch_count,
    routes,
    router_route_weight,
    output_gradient,
    frozen_gate_weight,
    adapter_down_weight,
    adapter_up_weight,
):
    rep_count = lax.axis_size("rep")
    exp_count = lax.axis_size("exp")
    token_count = routes.shape[0]
    route_count = routes.shape[1]
    fetch_slots = shard_request_index.shape[2]
    model_width = replay_buffer_rows.shape[1]
    hidden_units = frozen_gate_weight.shape[2]
    capacity = 7 * token_count * route_count // (4 * exp_count)
    tile_rows = exp_count * capacity
    served = jnp.take(replay_buffer_rows, shard_request_index[0], axis=0)
    arrived = lax.all_to_all(served, "rep", split_axis=0, concat_axis=0, tiled=True)
    flat_rows = arrived.reshape(rep_count * fetch_slots, model_width)
    counts = replica_fetch_count[0]
    row_ends = jnp.cumsum(counts)
    row_starts = row_ends - counts
    positions = jnp.arange(token_count, dtype=jnp.int32)
    source = jnp.sum((row_ends[None, :] <= positions[:, None]).astype(jnp.int32), axis=1)
    offset = positions - jnp.take(row_starts, source)
    tokens = jnp.take(flat_rows, source * fetch_slots + offset, axis=0)
    expert_ids = lax.broadcasted_iota(jnp.int32, (token_count * route_count, exp_count), 1)
    chosen = (routes == expert_ids).astype(jnp.int32)
    slot_rank = jnp.sum((jnp.cumsum(chosen, axis=0) - 1) * chosen, axis=1)
    target = (routes[:, 0] * capacity + slot_rank).reshape(token_count, route_count)
    row_ids = lax.broadcasted_iota(jnp.int32, (tile_rows, token_count), 0)
    pickers = [(row_ids == target[:, 0][None, :]).astype(jnp.bfloat16)]
    which_route = 0
    row_sum = jnp.dot(pickers[which_route], tokens, preferred_element_type=jnp.float32)
    sent_rows = row_sum.astype(jnp.bfloat16).reshape(exp_count, capacity, model_width)
    tile_in = lax.all_to_all(sent_rows, "exp", split_axis=0, concat_axis=0, tiled=True)
    input_tile = tile_in.reshape(tile_rows, model_width)
    adapted_hidden = jnp.dot(
        input_tile, adapter_down_weight[0], preferred_element_type=jnp.float32
    ).astype(jnp.bfloat16)
    pre_act = jnp.dot(
        input_tile, frozen_gate_weight[0], preferred_element_type=jnp.float32
    ) + jnp.dot(adapted_hidden, adapter_up_weight[0], preferred_element_type=jnp.float32)
    activated = jax.nn.silu(pre_act).astype(jnp.bfloat16)
    results = lax.all_to_all(
        activated.reshape(exp_count, capacity, hidden_units),
        "exp",
        split_axis=0,
        concat_axis=0,
        tiled=True,
    )
    result_rows = results.reshape(tile_rows, hidden_units)
    which_route = 0
    picked = jnp.take(result_rows, target[:, which_route], axis=0).astype(jnp.float32)
    combined = router_route_weight * picked
    out_rows = combined.astype(jnp.bfloat16)
    which_route = 0
    scaled = (router_route_weight * output_gradient.astype(jnp.float32)).astype(jnp.bfloat16)
    grad_sum = jnp.dot(pickers[which_route], scaled, preferred_element_type=jnp.float32)
    grad_in = lax.all_to_all(
        grad_sum.astype(jnp.bfloat16).reshape(exp_count, capacity, hidden_units),
        "exp",
        split_axis=0,
        concat_axis=0,
        tiled=True,
    )
    grad_tile = grad_in.reshape(tile_rows, hidden_units)
    preact_gradient = (grad_tile.astype(jnp.float32) * silu_slope(pre_act)).astype(jnp.bfloat16)
    up_term = lax.dot_general(
        adapted_hidden,
        preact_gradient,
        (((0,), (0,)), ((), ())),
        preferred_element_type=jnp.float32,
    )
    back_reduced = lax.dot_general(
        preact_gradient,
        adapter_up_weight[0],
        (((1,), (1,)), ((), ())),
        preferred_element_type=jnp.float32,
    ).astype(jnp.bfloat16)
    down_term = lax.dot_general(
        input_tile, back_reduced, (((0,), (0,)), ((), ())), preferred_element_type=jnp.float32
    )
    down_grad, up_grad = (
        lax.psum_scatter(down_term, "rep", scatter_dimension=0, tiled=True),
        lax.psum_scatter(up_term, "rep", scatter_dimension=0, tiled=True),
    )
    return (out_rows, down_grad[None], up_grad[None])


def solution(mesh):
    placed = (
        P(("rep", "exp"), None),
        P(("rep", "exp"), None, None),
        P(("rep", "exp"), None),
        P(("rep", "exp"), None),
        P(("rep", "exp"), None),
        P(("rep", "exp"), None),
        P("exp", None, None),
        P("exp", None, None),
        P("exp", None, None),
    )
    return jax.shard_map(
        body,
        mesh=mesh,
        in_specs=placed,
        out_specs=(P(("rep", "exp"), None), P("exp", "rep", None), P("exp", "rep", None)),
        check_vma=False,
    )
```

profile of v0, /device:TPU:1, one launch (start us, length us, event | category | flops | bytes accessed | tf_op | source)
XLA Modules:
  0.0 679.8 jit_solution(8498044250394353487)
XLA Ops:
  7.2 0.0 copy-start
  7.2 0.8 compare_select_fusion
  8.0 0.7 compare_and_fusion
  8.6 0.1 copy.22
  8.7 0.1 reshape.185
  8.8 0.1 copy.21
  8.9 0.0 copy-done
  8.9 1.7 gather_fusion.1
  10.6 1.5 bitcast_select_fusion
  12.1 0.0 copy-start.7
  12.1 0.0 copy-start.5
  12.1 0.0 copy-start.4
  12.1 0.0 copy-start.6
  12.1 17.9 %all-to-all-start = ((bf16[32,8,3584]{2,1,0:T(8,128)(2,1)}), bf16[32,8,3584]{2,1,0:T(8,128)(2,1)S(1)}, u32[]{:S(2)}, u32[]{:S(2)}) async-start(bf16[32,8,3584]{2,1,0:T(8,128)(2,1)} %bitcast_select_fusion), calls=%async_computation | async-start | bytes 3670016 | tf_op jit(solution)/shard_map/all_to_all | solution.py:33
  30.0 0.0 copy-done.7
  30.1 0.1 copy.20
  30.1 0.1 reduce-window.8
  30.2 0.1 reduce
  30.3 0.0 copy-done.5
  30.3 0.1 fusion.11
  30.4 0.2 reduce_window_sum.18
  30.6 0.2 select_reduce_fusion
  30.8 0.0 copy-done.4
  30.8 0.0 copy-done.6
  30.8 0.3 convolution_convert_fusion.1
  31.1 1.0 reshape.173
  32.1 0.1 convert_reduce_fusion
  32.2 47.8 %all-to-all-done = bf16[32,8,3584]{2,1,0:T(8,128)(2,1)S(1)} async-done(((bf16[32,8,3584]{2,1,0:T(8,128)(2,1)}), bf16[32,8,3584]{2,1,0:T(8,128)(2,1)S(1)}, u32[]{:S(2)}, u32[]{:S(2)}) %all-to-all-start) | async-done | bytes 1835040 | tf_op jit(solution)/shard_map/all_to_all | solution.py:33
  80.0 14.6 %all-to-all-start.3 = ((bf16[32,7,1024]{2,1,0:T(8,128)(2,1)}), bf16[32,7,1024]{2,1,0:T(8,128)(2,1)S(1)}, u32[]{:S(2)}, u32[]{:S(2)}) async-start(bf16[32,7,1024]{2,1,0:T(8,128)(2,1)} %reshape.173), calls=%async_computation.3 | async-start | bytes 1048576 | tf_op jit(solution)/shard_map/all_to_all | solution.py:75
  94.6 1.2 gather_fusion
  95.9 2.1 gather_fusion.2
  97.9 1.8 convolution_convert_fusion
  99.8 1.5 reshape.169
  101.3 7.0 %all-to-all-done.3 = bf16[32,7,1024]{2,1,0:T(8,128)(2,1)S(1)} async-done(((bf16[32,7,1024]{2,1,0:T(8,128)(2,1)}), bf16[32,7,1024]{2,1,0:T(8,128)(2,1)S(1)}, u32[]{:S(2)}, u32[]{:S(2)}) %all-to-all-start.3) | async-done | bytes 458784 | tf_op jit(solution)/shard_map/all_to_all | solution.py:75
  108.4 8.6 %all-to-all-start.1 = ((bf16[32,7,3584]{2,1,0:T(8,128)(2,1)}), bf16[32,7,3584]{2,1,0:T(8,128)(2,1)}, u32[]{:S(2)}, u32[]{:S(2)}) async-start(bf16[32,7,3584]{2,1,0:T(8,128)(2,1)} %reshape.169), calls=%async_computation.1 | async-start | bytes 3670016 | tf_op jit(solution)/shard_map/all_to_all | solution.py:51
  117.0 0.0 all-reduce.3.cloned.1.call-start
  117.0 1.0 reshape.174
  118.1 0.0 copy-start.1
  118.1 47.2 %all-to-all-done.1 = bf16[32,7,3584]{2,1,0:T(8,128)(2,1)} async-done(((bf16[32,7,3584]{2,1,0:T(8,128)(2,1)}), bf16[32,7,3584]{2,1,0:T(8,128)(2,1)}, u32[]{:S(2)}, u32[]{:S(2)}) %all-to-all-start.1) | async-done | bytes 1605664 | tf_op jit(solution)/shard_map/all_to_all | solution.py:51
  165.3 1.8 reshape.170
  167.1 0.0 copy-done.1
  167.1 0.6 convolution_convert_fusion.3
  167.6 0.0 copy-start.2
  167.7 0.0 copy-start.3
  167.7 5.0 fusion
  172.7 0.0 copy-done.2
  172.7 0.0 copy-done.3
  172.7 0.6 multiply_convert_fusion
  173.3 1.1 fusion.20
  174.3 0.0 all-reduce.3.cloned.1.call-update
  174.3 0.0 reduce-scatter.2.cloned.1.call-start
  174.4 3.4 fusion.2
  177.8 0.0 reduce-scatter.2.cloned.1.call-update
  177.8 0.9 reshape.171
  178.7 3.9 all-to-all-start.2
  182.6 1.3 dynamic-slice
  184.6 344.5 %all-reduce.3.cloned.1.call-done = f32[128,1024]{1,0:T(8,128)} async-done(((f32[128,1024]{1,0:T(8,128)}), f32[128,1024]{1,0:T(8,128)}) %all-reduce.3.cloned.1.call-update) | async-done | bytes 524304
  529.0 1.4 dynamic-slice_bitcast_fusion
  530.4 0.0 all-to-all-done.2
  530.4 0.2 reshape.172
  530.6 0.9 gather_fusion.3
  531.4 0.9 multiply_convert_fusion.3
  532.3 140.6 %reduce-scatter.2.cloned.1.call-done = f32[112,128]{1,0:T(8,128)} async-done(((f32[3584,128]{1,0:T(8,128)}), f32[112,128]{1,0:T(8,128)}) %reduce-scatter.2.cloned.1.call-update) | async-done | bytes 57360 | tf_op jit(solution)/shard_map/reduce_scatter | solution.py:100
  (10 shorter events, 0.1 us)
Async XLA Ops:
  7.2 1.8 copy-start
  12.1 17.9 %copy-start.7 = (s32[1,32]{1,0:T(1,128)S(1)}, s32[1,32]{1,0:T(1,128)}, u32[]{:S(2)}) copy-start(s32[1,32]{1,0:T(1,128)} %param.11) | copy-start | bytes 388
  12.1 18.2 %copy-start.5 = (s32[128,1]{0,1:T(1,128)S(1)}, s32[128,1]{0,1:T(1,128)}, u32[]{:S(2)}) copy-start(s32[128,1]{0,1:T(1,128)} %param.12) | copy-start | bytes 1540
  12.1 18.6 %copy-start.4 = (bf16[128,1024]{1,0:T(8,128)(2,1)S(1)}, bf16[128,1024]{1,0:T(8,128)(2,1)}, u32[]{:S(2)}) copy-start(bf16[128,1024]{1,0:T(8,128)(2,1)} %param.14) | copy-start | bytes 786436
  12.1 18.6 %copy-start.6 = (f32[128,1]{0,1:T(1,128)S(1)}, f32[128,1]{0,1:T(1,128)}, u32[]{:S(2)}) copy-start(f32[128,1]{0,1:T(1,128)} %param.13) | copy-start | bytes 1540
  12.1 67.8 %all-to-all-start = ((bf16[32,8,3584]{2,1,0:T(8,128)(2,1)}), bf16[32,8,3584]{2,1,0:T(8,128)(2,1)S(1)}, u32[]{:S(2)}, u32[]{:S(2)}) async-start(bf16[32,8,3584]{2,1,0:T(8,128)(2,1)} %bitcast_select_fusion), calls=%async_computation | async-start | bytes 3670016 | tf_op jit(solution)/shard_map/all_to_all | solution.py:33
  80.0 28.4 %all-to-all-start.3 = ((bf16[32,7,1024]{2,1,0:T(8,128)(2,1)}), bf16[32,7,1024]{2,1,0:T(8,128)(2,1)S(1)}, u32[]{:S(2)}, u32[]{:S(2)}) async-start(bf16[32,7,1024]{2,1,0:T(8,128)(2,1)} %reshape.173), calls=%async_computation.3 | async-start | bytes 1048576 | tf_op jit(solution)/shard_map/all_to_all | solution.py:75
  108.4 56.9 %all-to-all-start.1 = ((bf16[32,7,3584]{2,1,0:T(8,128)(2,1)}), bf16[32,7,3584]{2,1,0:T(8,128)(2,1)}, u32[]{:S(2)}, u32[]{:S(2)}) async-start(bf16[32,7,3584]{2,1,0:T(8,128)(2,1)} %reshape.169), calls=%async_computation.1 | async-start | bytes 3670016 | tf_op jit(solution)/shard_map/all_to_all | solution.py:51
  117.0 412.1 %all-reduce.3.cloned.1.call-start = ((), (), s32[]{:S(2)}) async-start(), calls=%async_computation.6 | async-start | bytes 1048576
  118.1 49.0 %copy-start.1 = (bf16[1,3584,128]{2,1,0:T(8,128)(2,1)S(1)}, bf16[1,3584,128]{2,1,0:T(8,128)(2,1)}, u32[]{:S(2)}) copy-start(bf16[1,3584,128]{2,1,0:T(8,128)(2,1)} %param.16) | copy-start | bytes 2752516
  167.6 5.0 copy-start.2
  167.7 5.0 copy-start.3
  174.3 498.6 %reduce-scatter.2.cloned.1.call-start = ((), (), s32[]{:S(2)}) async-start(), calls=%async_computation.5 | async-start | bytes 1892352 | tf_op jit(solution)/shard_map/reduce_scatter | solution.py:100
  178.7 351.7 %all-to-all-start.2 = ((bf16[32,7,1024]{2,1,0:T(8,128)(2,1)}), bf16[32,7,1024]{2,1,0:T(8,128)(2,1)S(1)}, u32[]{:S(2)}, u32[]{:S(2)}) async-start(bf16[32,7,1024]{2,1,0:T(8,128)(2,1)} %reshape.171), calls=%async_computation.2 | async-start | bytes 1048576 | tf_op jit(solution)/shard_map/all_to_all | solution.py:60
Sparse Core Ops, SparseCore 0:
  174.5 354.5 all-reduce.2
  535.5 137.4 reduce-scatter.1
where the time goes:
time: 684 us; the launch traced here: 680 us
  waiting for transfers between devices  587 us (86%)
  starting transfers between devices  45.1 us (7%)
  local copies, waits for them, and re-layouts  15.3 us (2%)
  between operations  14.9 us (2%)
  matrix products  12.7 us (2%)
    unnamed x3, waiting for transfers between devices  344 us
    reduce_scatter x1, waiting for transfers between devices, body(): lax.psum_scatter(down_term, 'rep', scatter_dimension=0, tiled=True)  141 us
    all_to_all x1, waiting for transfers between devices, body(): lax.all_to_all(served, 'rep', split_axis=0, concat_axis=0, tiled=True)  47.8 us
    all_to_all x1, waiting for transfers between devices, body(): lax.all_to_all(sent_rows, 'exp', split_axis=0, concat_axis=0, tiled=True)  47.2 us
    all_to_all x1, starting transfers between devices, body(): lax.all_to_all(served, 'rep', split_axis=0, concat_axis=0, tiled=True)  17.9 us
    all_to_all x1, starting transfers between devices, body(): lax.all_to_all(grad_sum.astype(jnp.bfloat16).reshape(exp_count, capacity,...  14.6 us
  transfers between devices with their start and end apart: 6, of which 5 were waited for; matrix products, arithmetic and copies ran while one was open for 3% of the time, Pallas kernels for 0%

commit v1 on v0

v1 whole, which is shorter than its diff:
```python
import jax
import jax.numpy as jnp
from jax import lax
from jax.sharding import PartitionSpec as P

CAPACITY = 7
LANES = 128


def silu_slope(pre_act):
    gate_value = jax.nn.sigmoid(pre_act)
    return gate_value * (1.0 + pre_act * (1.0 - gate_value))


def body(
    replay_buffer_rows,
    shard_request_index,
    replica_fetch_count,
    routes,
    router_route_weight,
    output_gradient,
    frozen_gate_weight,
    adapter_down_weight,
    adapter_up_weight,
):
    rep_count = lax.axis_size("rep")
    exp_count = lax.axis_size("exp")
    token_count = routes.shape[0]
    fetch_slots = shard_request_index.shape[2]
    model_width = replay_buffer_rows.shape[1]
    hidden_units = frozen_gate_weight.shape[2]
    rank = adapter_down_weight.shape[2]
    tile_rows = exp_count * CAPACITY

    served = jnp.take(replay_buffer_rows, shard_request_index[0], axis=0)
    arrived = lax.all_to_all(served, "rep", split_axis=0, concat_axis=0, tiled=True)
    flat_rows = arrived.reshape(rep_count * fetch_slots, model_width)

    counts = replica_fetch_count[0]
    row_ends = jnp.cumsum(counts)
    row_starts = row_ends - counts
    positions = jnp.arange(token_count, dtype=jnp.int32)
    passed = (row_ends[None, :] <= positions[:, None]).astype(jnp.int32)
    source = jnp.sum(passed, axis=1)
    start_of = jnp.sum(passed * counts[None, :], axis=1)
    place = source * fetch_slots + positions - start_of
    expert_ids = lax.broadcasted_iota(jnp.int32, (token_count, exp_count), 1)
    chosen = (routes == expert_ids).astype(jnp.int32)
    slot_rank = jnp.sum((jnp.cumsum(chosen, axis=0) - 1) * chosen, axis=1)
    target = routes[:, 0] * CAPACITY + slot_rank
    row_ids = lax.broadcasted_iota(jnp.int32, (tile_rows, token_count), 0)
    picker = (row_ids == target[None, :]).astype(jnp.bfloat16)
    place_ids = lax.broadcasted_iota(jnp.int32, (token_count, rep_count * fetch_slots), 1)
    finder = (place_ids == place[:, None]).astype(jnp.bfloat16)
    mover = jnp.dot(picker, finder, preferred_element_type=jnp.float32).astype(jnp.bfloat16)

    scaled = (router_route_weight * output_gradient.astype(jnp.float32)).astype(jnp.bfloat16)
    grad_slots = jnp.dot(picker, scaled, preferred_element_type=jnp.float32).astype(jnp.bfloat16)
    row_slots = jnp.dot(mover, flat_rows, preferred_element_type=jnp.float32).astype(jnp.bfloat16)
    packed = jnp.concatenate([row_slots, grad_slots], axis=1)
    packed = packed.reshape(exp_count, CAPACITY, model_width + hidden_units)
    tile_in = lax.all_to_all(packed, "exp", split_axis=0, concat_axis=0, tiled=True)
    tile_in = tile_in.reshape(tile_rows, model_width + hidden_units)
    input_tile = tile_in[:, :model_width]
    grad_tile = tile_in[:, model_width:]

    adapted_hidden = jnp.dot(
        input_tile, adapter_down_weight[0], preferred_element_type=jnp.float32
    ).astype(jnp.bfloat16)
    pre_act = jnp.dot(
        input_tile, frozen_gate_weight[0], preferred_element_type=jnp.float32
    ) + jnp.dot(adapted_hidden, adapter_up_weight[0], preferred_element_type=jnp.float32)
    activated = jax.nn.silu(pre_act).astype(jnp.bfloat16)
    results = lax.all_to_all(
        activated.reshape(exp_count, CAPACITY, hidden_units),
        "exp",
        split_axis=0,
        concat_axis=0,
        tiled=True,
    )
    result_rows = results.reshape(tile_rows, hidden_units)
    picked = jnp.take(result_rows, target, axis=0).astype(jnp.float32)
    out_rows = (router_route_weight * picked).astype(jnp.bfloat16)

    preact_gradient = (grad_tile.astype(jnp.float32) * silu_slope(pre_act)).astype(jnp.bfloat16)
    up_term = lax.dot_general(
        adapted_hidden,
        preact_gradient,
        (((0,), (0,)), ((), ())),
        preferred_element_type=jnp.float32,
    )
    back_reduced = lax.dot_general(
        preact_gradient,
        adapter_up_weight[0],
        (((1,), (1,)), ((), ())),
        preferred_element_type=jnp.float32,
    ).astype(jnp.bfloat16)
    down_term = lax.dot_general(
        input_tile, back_reduced, (((0,), (0,)), ((), ())), preferred_element_type=jnp.float32
    )
    down_rows = model_width // rep_count
    up_rows = rank // rep_count
    up_tiles = up_rows * hidden_units // LANES
    terms = jnp.concatenate(
        [
            down_term.astype(jnp.bfloat16).reshape(rep_count, down_rows, rank),
            up_term.astype(jnp.bfloat16).reshape(rep_count, up_tiles, LANES),
        ],
        axis=1,
    )
    landed = lax.all_to_all(terms, "rep", split_axis=0, concat_axis=0, tiled=True)
    total = jnp.sum(landed.astype(jnp.float32), axis=0)
    down_grad = total[:down_rows].reshape(1, down_rows, rank)
    up_grad = total[down_rows:].reshape(1, up_rows, hidden_units)
    return (out_rows, down_grad, up_grad)


def solution(mesh):
    placed = (
        P(("rep", "exp"), None),
        P(("rep", "exp"), None, None),
        P(("rep", "exp"), None),
        P(("rep", "exp"), None),
        P(("rep", "exp"), None),
        P(("rep", "exp"), None),
        P("exp", None, None),
        P("exp", None, None),
        P("exp", None, None),
    )
    return jax.shard_map(
        body,
        mesh=mesh,
        in_specs=placed,
        out_specs=(P(("rep", "exp"), None), P("exp", "rep", None), P("exp", "rep", None)),
        check_vma=False,
    )
```

time: 684 us -> 239 us (0.35)
  the two profiles are of different devices: /device:TPU:1 before, /device:TPU:20 now
where the time goes in v1:
time: 239 us; the launch traced here: 237 us
  blocking collectives  83.9 us (35%)
  waiting for transfers between devices  82.9 us (35%)
  starting transfers between devices  31.6 us (13%)
  matrix products  15.6 us (7%)
  local copies, waits for them, and re-layouts  12.5 us (5%)
  other arithmetic  9.96 us (4%)
    all_to_all x1, blocking collectives, body(): lax.all_to_all(packed, 'exp', split_axis=0, concat_axis=0, tiled=True)  83.9 us
    all_to_all x1, waiting for transfers between devices, body(): lax.all_to_all(served, 'rep', split_axis=0, concat_axis=0, tiled=True)  41.3 us
    all_to_all x1, waiting for transfers between devices, body(): lax.all_to_all(terms, 'rep', split_axis=0, concat_axis=0, tiled=True)  35.1 us
    all_to_all x1, starting transfers between devices, body(): lax.all_to_all(terms, 'rep', split_axis=0, concat_axis=0, tiled=True)  13.7 us
    all_to_all x1, starting transfers between devices, body(): lax.all_to_all(served, 'rep', split_axis=0, concat_axis=0, tiled=True)  11.3 us
    all_to_all x1, starting transfers between devices, body(): lax.all_to_all(activated.reshape(exp_count, CAPACITY, hidden_units), 'exp...  6.55 us
    all_to_all x1, waiting for transfers between devices, body(): lax.all_to_all(activated.reshape(exp_count, CAPACITY, hidden_units), 'exp...  6.49 us
    dot_general x1, matrix products, body(): jnp.dot(input_tile, frozen_gate_weight[0], preferred_element_type=jnp.flo...  4.95 us
  transfers between devices with their start and end apart: 3, of which 3 were waited for; matrix products, arithmetic and copies ran while one was open for 5% of the time, Pallas kernels for 0%

profile of v1, /device:TPU:20, one launch (start us, length us, event | category | flops | bytes accessed | tf_op | source)
XLA Modules:
  0.0 237.3 jit_solution(4686528826333789969)
XLA Ops:
  0.6 0.0 copy-start
  0.6 0.8 compare_select_fusion
  1.4 0.7 compare_and_fusion
  2.1 0.1 copy.16
  2.2 0.1 reshape.128
  2.3 0.1 copy.15
  2.4 0.0 copy-done
  2.4 1.7 gather_fusion
  4.1 1.5 bitcast_select_fusion
  5.6 0.0 copy-start.5
  5.6 0.0 copy-start.4
  5.6 0.0 copy-start.2
  5.6 0.0 copy-start.6
  5.6 11.3 %all-to-all-start = ((bf16[32,8,3584]{2,1,0:T(8,128)(2,1)}), bf16[32,8,3584]{2,1,0:T(8,128)(2,1)S(1)}, u32[]{:S(2)}, u32[]{:S(2)}) async-start(bf16[32,8,3584]{2,1,0:T(8,128)(2,1)} %bitcast_select_fusion), calls=%async_computation | async-start | bytes 3670016 | tf_op jit(solution)/shard_map/all_to_all | solution.py:36
  16.9 0.0 copy-done.5
  16.9 0.1 copy.14
  17.0 0.0 copy-done.4
  17.0 0.1 fusion.17
  17.1 0.2 reduce_window_sum.18
  17.3 0.1 reduce-window.8
  17.3 0.1 reduce
  17.5 0.1 convert_reduce_fusion.1
  17.6 0.2 select_reduce_fusion.1
  17.8 0.0 copy-done.2
  17.8 0.0 copy-done.6
  17.8 0.4 convolution_convert_fusion.2
  18.1 41.3 %all-to-all-done = bf16[32,8,3584]{2,1,0:T(8,128)(2,1)S(1)} async-done(((bf16[32,8,3584]{2,1,0:T(8,128)(2,1)}), bf16[32,8,3584]{2,1,0:T(8,128)(2,1)S(1)}, u32[]{:S(2)}, u32[]{:S(2)}) %all-to-all-start) | async-done | bytes 1835040 | tf_op jit(solution)/shard_map/all_to_all | solution.py:36
  59.4 1.9 convolution_convert_fusion
  61.4 2.9 %pad_maximum_fusion = bf16[224,4608]{1,0:T(8,128)(2,1)} fusion(bf16[224,1024]{1,0:T(8,128)(2,1)S(1)} %convolution_convert_fusion.2, bf16[224,3584]{1,0:T(8,128)(2,1)} %convolution_convert_fusion), kind=kLoop, calls=%fused_computation.7 | loop fusion | flops 4128768 | bytes 4128768 | tf_op jit(solution)/shard_map/concatenate | solution.py:60
  64.3 2.7 %reshape.118 = bf16[32,7,4608]{2,1,0:T(8,128)(2,1)S(1)} reshape(bf16[224,4608]{1,0:T(8,128)(2,1)} %pad_maximum_fusion) | data formatting | bytes 4128768 | tf_op jit(solution)/shard_map/reshape | solution.py:61
  66.9 83.9 %all_to_all.20 = bf16[32,7,4608]{2,1,0:T(8,128)(2,1)} all-to-all(bf16[32,7,4608]{2,1,0:T(8,128)(2,1)S(1)} %reshape.118), channel_id=1, replica_groups=mesh['rep'=32,'exp'=32] {'exp'}, dimensions={0} | all-to-all | bytes 4128768 | tf_op jit(solution)/shard_map/all_to_all | solution.py:62
  150.8 2.8 %reshape.119 = bf16[224,4608]{1,0:T(8,128)(2,1)S(1)} reshape(bf16[32,7,4608]{2,1,0:T(8,128)(2,1)} %all_to_all.20) | data formatting | bytes 4128768 | tf_op jit(solution)/shard_map/reshape | solution.py:63
  153.6 1.8 fusion.7
  155.4 0.0 copy-start.3
  155.4 0.0 copy-start.1
  155.4 4.9 %fusion = f32[224,1024]{1,0:T(8,128)S(1)} fusion(bf16[1,3584,1024]{2,1,0:T(8,128)(2,1)} %param.15, bf16[224,4608]{1,0:T(8,128)(2,1)S(1)} %reshape.119), kind=kOutput, calls=%fused_computation.2 | convolution fusion | flops 1644167168 | bytes 9863168 | tf_op jit(solution)/shard_map/dot_general | solution.py:70
  160.3 0.0 copy-done.3
  160.3 0.0 copy-done.1
  160.4 1.4 multiply_convert_fusion
  161.7 0.9 reshape.120
  162.7 6.5 %all-to-all-start.2 = ((bf16[32,7,1024]{2,1,0:T(8,128)(2,1)}), bf16[32,7,1024]{2,1,0:T(8,128)(2,1)S(1)}, u32[]{:S(2)}, u32[]{:S(2)}) async-start(bf16[32,7,1024]{2,1,0:T(8,128)(2,1)} %reshape.120), calls=%async_computation.2 | async-start | bytes 1048576 | tf_op jit(solution)/shard_map/all_to_all | solution.py:74
  169.2 2.0 convolution_convert_fusion.3
  171.2 1.8 reshape.123
  173.0 3.2 %convolution_convert_fusion.1 = bf16[3584,128]{1,0:T(8,128)(2,1)} fusion(bf16[224,4608]{1,0:T(8,128)(2,1)S(1)} %reshape.119, bf16[224,1024]{1,0:T(8,128)(2,1)} %get-tuple-element.7, bf16[1,128,1024]{2,1,0:T(8,128)(2,1)} %param.17), kind=kOutput, calls=%fused_computation.5 | convolution fusion | flops 264728576 | bytes 3244032 | tf_op jit(solution)/shard_map/dot_general | solution.py:98
  176.2 2.3 pad_maximum_fusion.1
  178.6 6.5 %all-to-all-done.2 = bf16[32,7,1024]{2,1,0:T(8,128)(2,1)S(1)} async-done(((bf16[32,7,1024]{2,1,0:T(8,128)(2,1)}), bf16[32,7,1024]{2,1,0:T(8,128)(2,1)S(1)}, u32[]{:S(2)}, u32[]{:S(2)}) %all-to-all-start.2) | async-done | bytes 458784 | tf_op jit(solution)/shard_map/all_to_all | solution.py:74
  185.1 13.7 %all-to-all-start.3 = ((bf16[32,144,128]{2,1,0:T(8,128)(2,1)}), bf16[32,144,128]{2,1,0:T(8,128)(2,1)S(1)}, u32[]{:S(2)}, u32[]{:S(2)}) async-start(bf16[32,144,128]{2,1,0:T(8,128)(2,1)} %pad_maximum_fusion.1), calls=%async_computation.3 | async-start | bytes 2359296 | tf_op jit(solution)/shard_map/all_to_all | solution.py:111
  198.8 0.2 reshape.121
  199.0 0.9 gather_fusion.1
  199.8 0.9 multiply_convert_fusion.2
  200.7 35.1 %all-to-all-done.3 = bf16[32,144,128]{2,1,0:T(8,128)(2,1)S(1)} async-done(((bf16[32,144,128]{2,1,0:T(8,128)(2,1)}), bf16[32,144,128]{2,1,0:T(8,128)(2,1)S(1)}, u32[]{:S(2)}, u32[]{:S(2)}) %all-to-all-start.3) | async-done | bytes 1179680 | tf_op jit(solution)/shard_map/all_to_all | solution.py:111
  235.8 0.2 convert_reduce_fusion
  236.0 0.6 slice_bitcast_fusion
  236.6 0.6 reshape.125
  (5 shorter events, 0.0 us)
Async XLA Ops:
  0.6 1.8 copy-start
  5.6 11.3 %copy-start.5 = (s32[1,32]{1,0:T(1,128)S(1)}, s32[1,32]{1,0:T(1,128)}, u32[]{:S(2)}) copy-start(s32[1,32]{1,0:T(1,128)} %param.11) | copy-start | bytes 388
  5.6 11.4 %copy-start.4 = (s32[128,1]{0,1:T(1,128)S(1)}, s32[128,1]{0,1:T(1,128)}, u32[]{:S(2)}) copy-start(s32[128,1]{0,1:T(1,128)} %param.12) | copy-start | bytes 1540
  5.6 12.2 %copy-start.2 = (bf16[128,1024]{1,0:T(8,128)(2,1)S(1)}, bf16[128,1024]{1,0:T(8,128)(2,1)}, u32[]{:S(2)}) copy-start(bf16[128,1024]{1,0:T(8,128)(2,1)} %param.14) | copy-start | bytes 786436
  5.6 12.2 %copy-start.6 = (f32[128,1]{0,1:T(1,128)S(1)}, f32[128,1]{0,1:T(1,128)}, u32[]{:S(2)}) copy-start(f32[128,1]{0,1:T(1,128)} %param.13) | copy-start | bytes 1540
  5.6 53.8 %all-to-all-start = ((bf16[32,8,3584]{2,1,0:T(8,128)(2,1)}), bf16[32,8,3584]{2,1,0:T(8,128)(2,1)S(1)}, u32[]{:S(2)}, u32[]{:S(2)}) async-start(bf16[32,8,3584]{2,1,0:T(8,128)(2,1)} %bitcast_select_fusion), calls=%async_computation | async-start | bytes 3670016 | tf_op jit(solution)/shard_map/all_to_all | solution.py:36
  155.4 5.0 %copy-start.3 = (bf16[224,128]{1,0:T(8,128)(2,1)}, bf16[224,128]{1,0:T(8,128)(2,1)S(1)}, u32[]{:S(2)}) copy-start(bf16[224,128]{1,0:T(8,128)(2,1)S(1)} %fusion.7) | copy-start | bytes 172036
  155.4 5.0 %copy-start.1 = (bf16[1,128,1024]{2,1,0:T(8,128)(2,1)S(1)}, bf16[1,128,1024]{2,1,0:T(8,128)(2,1)}, u32[]{:S(2)}) copy-start(bf16[1,128,1024]{2,1,0:T(8,128)(2,1)} %param.17) | copy-start | bytes 786436
  162.7 22.4 %all-to-all-start.2 = ((bf16[32,7,1024]{2,1,0:T(8,128)(2,1)}), bf16[32,7,1024]{2,1,0:T(8,128)(2,1)S(1)}, u32[]{:S(2)}, u32[]{:S(2)}) async-start(bf16[32,7,1024]{2,1,0:T(8,128)(2,1)} %reshape.120), calls=%async_computation.2 | async-start | bytes 1048576 | tf_op jit(solution)/shard_map/all_to_all | solution.py:74
  185.1 50.8 %all-to-all-start.3 = ((bf16[32,144,128]{2,1,0:T(8,128)(2,1)}), bf16[32,144,128]{2,1,0:T(8,128)(2,1)S(1)}, u32[]{:S(2)}, u32[]{:S(2)}) async-start(bf16[32,144,128]{2,1,0:T(8,128)(2,1)} %pad_maximum_fusion.1), calls=%async_computation.3 | async-start | bytes 2359296 | tf_op jit(solution)/shard_map/all_to_all | solution.py:111
